TPU v7x, 32 devices: a whole 2x2x4 slice. The times are simulated.
32 devices in a mesh: section: 2 (over core), dom: 16 (over z, y, x).
Axes of the slice: x: 2, y: 2, z: 4, core: 2. Of those that a mesh axis runs over, the one named last changes fastest.
Arguments:
- blocks: float32 [16, 32, 6, 128, 128], P('section', 'dom'), may hold values from -0.21875 to 0.21875
- column_index: int32 [16, 32, 6], P('section', 'dom'), may hold values from 0 to 31
- block_period: int32 [16, 32, 6], P('section', 'dom'), may hold values from 0 to 15, as said below
- cost_vector: float32 [16, 4096], P('section', 'dom'), may hold values from -6 to 6
- demand: float32 [16, 4096], P('section', 'dom'), may hold values from -12 to 12
- primal_start: float32 [16, 4096], P('section', 'dom'), may hold values from 0 to 2
- dual_start: float32 [16, 4096], P('section', 'dom'), may hold values from -3 to 3
- primal_weight: float32 [1], replicated, may hold values from 0.5 to 2
Outputs:
- primal_final: float32 [16, 4096], P('section', 'dom')
- dual_final: float32 [16, 4096], P('section', 'dom')
Inputs may be any that keep to these rules, and one draw needn't show every extreme that they name: block_period[p, r, k] is p or p - 1; it is p for k = 0 and for p = 0.
All inputs are finite; a program needn't handle non-finite values.
Results may differ from a plain program's by a relative error of at most 0.00011.
Values sent between devices are 32-bit elements; how exact they have to be, the bound alone decides.
A program may use at most 64 MiB of HBM per device.

v0:
```python
import jax
import jax.numpy as jnp
from jax import lax
from jax.sharding import PartitionSpec as P

step_scale = 0.4
epsilon = 1e-06


def passed_along(block, axis, distance):
    devices = range(lax.axis_size(axis))
    route = [(i - distance, i) for i in devices if i - distance in devices]
    return lax.ppermute(block, axis, route)


def slot_layout(column_index, block_period):
    periods_here = column_index.shape[0]
    local_period = jnp.arange(periods_here, dtype=jnp.int32)[:, None, None]
    global_period = lax.axis_index("section") * periods_here + local_period
    slot_index = local_period + block_period - global_period + 1
    return slot_index


def forward(blocks, column_index, slot_index, field):
    periods_here = field.shape[0]
    width_here = blocks.shape[-1]
    gathered = lax.all_gather(field, "dom", axis=1, tiled=True)
    carried = passed_along(gathered[-1:], "section", 1)
    stacked = jnp.concatenate([carried, gathered], axis=0)
    block_count = stacked.shape[1] // width_here
    picked = stacked.reshape(periods_here + 1, block_count, width_here)[slot_index, column_index]
    product = jnp.einsum("prkij,prkj->pri", blocks, picked, precision=lax.Precision.HIGHEST)
    return product.reshape(periods_here, -1)


def adjoint(blocks, column_index, slot_index, field):
    periods_here = field.shape[0]
    rows_here = blocks.shape[1]
    width_here = blocks.shape[-1]
    block_count = rows_here * lax.axis_size("dom")
    field_blocks = field.reshape(periods_here, rows_here, width_here)
    block_terms = jnp.einsum(
        "prkij,pri->prkj", blocks, field_blocks, precision=lax.Precision.HIGHEST
    )
    segment_ids = (slot_index * block_count + column_index).reshape(-1)
    dense_term = jax.ops.segment_sum(
        block_terms.reshape(-1, width_here),
        segment_ids,
        num_segments=(periods_here + 1) * block_count,
    )
    dense_term = dense_term.reshape(periods_here + 1, block_count * width_here)
    carried = passed_along(dense_term[:1], "section", -1)
    own_rows = dense_term[1:]
    merged = own_rows + jnp.concatenate([jnp.zeros_like(own_rows[:-1]), carried], axis=0)
    result = lax.psum_scatter(merged, "dom", scatter_dimension=1, tiled=True)
    return result


def on_device(
    blocks, column_index, block_period, cost_vector, demand, primal_start, dual_start, primal_weight
):
    slot_index = slot_layout(column_index, block_period)
    weight_now = primal_weight[0]
    tau_first = step_scale / weight_now
    sigma_first = step_scale * weight_now
    primal_one = jnp.maximum(
        0.0,
        primal_start
        - tau_first * (cost_vector - adjoint(blocks, column_index, slot_index, dual_start)),
    )
    dual_one = dual_start + sigma_first * (
        demand - forward(blocks, column_index, slot_index, 2.0 * primal_one - primal_start)
    )
    local_primal = jnp.sum((primal_one - primal_start) ** 2)
    local_dual = jnp.sum((dual_one - dual_start) ** 2)
    move_primal, move_dual = lax.psum((local_primal, local_dual), ("section", "dom"))
    weight_next = jnp.sqrt(weight_now * jnp.sqrt((move_dual + epsilon) / (move_primal + epsilon)))
    tau_second = step_scale / weight_next
    sigma_second = step_scale * weight_next
    primal_final = jnp.maximum(
        0.0,
        primal_one
        - tau_second * (cost_vector - adjoint(blocks, column_index, slot_index, dual_one)),
    )
    dual_final = dual_one + sigma_second * (
        demand - forward(blocks, column_index, slot_index, 2.0 * primal_final - primal_one)
    )
    return (primal_final, dual_final)


def solution(mesh):
    return jax.shard_map(
        on_device,
        mesh=mesh,
        in_specs=(
            P("section", "dom", None, None, None),
            P("section", "dom", None),
            P("section", "dom", None),
            P("section", "dom"),
            P("section", "dom"),
            P("section", "dom"),
            P("section", "dom"),
            P(),
        ),
        out_specs=(P("section", "dom"), P("section", "dom")),
        check_vma=False,
    )
```

profile of v0, /device:TPU:0, one launch (start us, length us, event | category | flops | bytes accessed | tf_op | source)
XLA Modules:
  0.0 288.4 jit_solution(15570511346201908841)
XLA Ops:
  7.2 0.0 copy-start.1
  7.2 0.0 copy-start.2
  7.2 0.0 reduce-scatter.3.cloned.1.call-start
  7.2 0.7 fusion.14
  8.0 0.1 copy.12
  8.1 0.1 reshape.61
  8.2 6.1 %fusion.10 = f32[8,2,1,6,128]{4,2,3,1,0:T(1,128)S(1)} fusion(f32[8,2,6,128,128]{4,3,2,1,0:T(8,128)} %param.8, f32[8,2,128,1,1]{2,0,1,3,4:T(8,128)} %bitcast.58), kind=kOutput, calls=%fused_computation.24 | convolution fusion | flops 18874368 | bytes 6348800 | tf_op jit(solution)/shard_map/prkij,pri->prkj/dot_general | solution.py:42
  14.3 0.0 copy-start
  14.3 0.0 copy-start.3
  14.3 0.9 scatter_custom_fusion
  15.2 1.3 collective-permute-start
  16.6 1.7 collective-permute-done
  18.3 0.7 pad_add_fusion.1
  19.0 0.0 reduce-scatter.3.cloned.1.call-update
  19.0 0.0 reduce-scatter.5.cloned.1.call-start
  19.8 78.9 %reduce-scatter.3.cloned.1.call-done = f32[8,256]{1,0:T(8,128)} async-done(((f32[8,4096]{1,0:T(8,128)}), f32[8,256]{1,0:T(8,128)}) %reduce-scatter.3.cloned.1.call-update) | async-done | bytes 8208 | tf_op jit(solution)/shard_map/reduce_scatter | solution.py:55
  98.7 0.0 copy-done.1
  98.7 0.0 copy-done.2
  98.7 1.3 multiply_reduce_fusion
  100.0 36.7 %all_gather.6 = f32[8,4096]{1,0:T(8,128)S(1)} all-gather(f32[8,256]{1,0:T(8,128)S(1)} %multiply_subtract_fusion.1), channel_id=1, replica_groups=mesh['section'=2,'dom'=16] {'dom'}, dimensions={1}, use_global_device_ids=true | all-gather | bytes 139264 | tf_op jit(solution)/shard_map/all_gather | solution.py:27
  136.7 1.3 collective-permute-start.1
  138.0 0.1 copy.13
  138.1 0.1 reshape.47
  138.2 0.6 collective-permute-done.1
  138.8 0.1 copy.22
  138.9 1.4 gather_fusion
  140.3 7.1 %fusion.18 = f32[8,2,1,128,1]{3,2,4,1,0:T(1,128)S(1)} fusion(f32[8,2,6,128,1]{3,4,2,1,0:T(1,128)S(1)} %bitcast.54, f32[8,2,6,128,128]{4,3,2,1,0:T(8,128)} %param.8), kind=kOutput, calls=%fused_computation.40 | convolution fusion | flops 18874368 | bytes 6348800 | tf_op jit(solution)/shard_map/prkij,prkj->pri/dot_general | solution.py:32
  147.4 0.0 copy-done
  147.4 0.0 copy-done.3
  147.4 0.7 multiply_reduce_fusion.1
  148.1 5.1 %fusion.8 = f32[8,2,1,6,128]{4,2,3,1,0:T(1,128)S(1)} fusion(f32[8,2,6,128,128]{4,3,2,1,0:T(8,128)} %param.8, f32[8,2,128,1,1]{2,0,1,3,4:T(8,128)S(1)} %bitcast.57), kind=kOutput, calls=%fused_computation.22 | convolution fusion | flops 18874368 | bytes 6348800 | tf_op jit(solution)/shard_map/prkij,pri->prkj/dot_general | solution.py:42
  153.2 0.9 scatter_custom_fusion.1
  154.1 1.3 collective-permute-start.2
  155.5 1.7 collective-permute-done.2
  157.2 0.7 pad_add_fusion
  157.9 0.0 reduce-scatter.5.cloned.1.call-update
  157.9 37.2 %all-reduce.2 = (f32[]{:T(128)}, f32[]{:T(128)}) all-reduce(f32[]{:T(128)} %get-tuple-element.8, f32[]{:T(128)} %get-tuple-element.6), channel_id=1, replica_groups=mesh['section'=2,'dom'=16] {'section','dom'}, use_global_device_ids=true, to_apply=%region_3.0 | all-reduce | flops 2 | bytes 16 | tf_op jit(solution)/shard_map/psum | solution.py:76
  196.5 35.8 %reduce-scatter.5.cloned.1.call-done = f32[8,256]{1,0:T(8,128)} async-done(((f32[8,4096]{1,0:T(8,128)}), f32[8,256]{1,0:T(8,128)}) %reduce-scatter.5.cloned.1.call-update) | async-done | bytes 8208 | tf_op jit(solution)/shard_map/reduce_scatter | solution.py:55
  232.3 1.3 multiply_subtract_fusion
  233.6 36.6 %all_gather.7 = f32[8,4096]{1,0:T(8,128)S(1)} all-gather(f32[8,256]{1,0:T(8,128)S(1)} %get-tuple-element.4), channel_id=1, replica_groups=mesh['section'=2,'dom'=16] {'dom'}, dimensions={1}, use_global_device_ids=true | all-gather | bytes 139264 | tf_op jit(solution)/shard_map/all_gather | solution.py:27
  270.3 1.5 collective-permute-start.3
  271.7 0.6 collective-permute-done.3
  272.4 0.1 copy.23
  272.5 1.4 gather_fusion.1
  273.9 7.1 %fusion.19 = f32[8,2,1,128,1]{3,2,4,1,0:T(1,128)S(1)} fusion(f32[8,2,6,128,1]{3,4,2,1,0:T(1,128)S(1)} %bitcast.53, f32[8,2,6,128,128]{4,3,2,1,0:T(8,128)} %param.8), kind=kOutput, calls=%fused_computation.41 | convolution fusion | flops 18874368 | bytes 6348800 | tf_op jit(solution)/shard_map/prkij,prkj->pri/dot_general | solution.py:32
  281.0 0.6 fusion.5
  (18 shorter events, 0.2 us)
Async XLA Ops:
  7.2 91.5 %copy-start.1 = (f32[8,256]{1,0:T(8,128)S(1)}, f32[8,256]{1,0:T(8,128)}, u32[]{:S(2)}) copy-start(f32[8,256]{1,0:T(8,128)} %param.13) | copy-start | bytes 24580
  7.2 91.5 %copy-start.2 = (f32[8,256]{1,0:T(8,128)S(1)}, f32[8,256]{1,0:T(8,128)}, u32[]{:S(2)}) copy-start(f32[8,256]{1,0:T(8,128)} %param.11) | copy-start | bytes 24580
  7.2 91.5 %reduce-scatter.3.cloned.1.call-start = ((), (), s32[]{:S(2)}) async-start(), calls=%async_computation.2 | async-start | bytes 139264 | tf_op jit(solution)/shard_map/reduce_scatter | solution.py:55
  14.3 133.1 %copy-start = (f32[8,256]{1,0:T(8,128)S(1)}, f32[8,256]{1,0:T(8,128)}, u32[]{:S(2)}) copy-start(f32[8,256]{1,0:T(8,128)} %param.14) | copy-start | bytes 24580
  14.3 133.1 %copy-start.3 = (f32[8,256]{1,0:T(8,128)S(1)}, f32[8,256]{1,0:T(8,128)}, u32[]{:S(2)}) copy-start(f32[8,256]{1,0:T(8,128)} %param.12) | copy-start | bytes 24580
  15.2 3.1 %collective-permute-start = (f32[1,4096]{1,0:T(1,128)S(1)}, f32[1,4096]{1,0:T(1,128)S(1)}, u32[]{:S(2)}, u32[]{:S(2)}) collective-permute-start(f32[1,4096]{1,0:T(1,128)S(1)} %bitcast.59), channel_id=1, source_target_pairs={{16,0},{17,1},{18,2},{19,3},{20,4},{21,5},{22,6},{23,7},{24,8},{25... | collective-permute-start | bytes 49160 | tf_op jit(solution)/shard_map/ppermute | solution.py:13
  19.0 213.3 %reduce-scatter.5.cloned.1.call-start = ((), (), s32[]{:S(2)}) async-start(), calls=%async_computation.3 | async-start | bytes 139264 | tf_op jit(solution)/shard_map/reduce_scatter | solution.py:55
  136.7 2.1 collective-permute-start.1
  154.1 3.1 %collective-permute-start.2 = (f32[1,4096]{1,0:T(1,128)S(1)}, f32[1,4096]{1,0:T(1,128)S(1)}, u32[]{:S(2)}, u32[]{:S(2)}) collective-permute-start(f32[1,4096]{1,0:T(1,128)S(1)} %bitcast.60), channel_id=1, source_target_pairs={{16,0},{17,1},{18,2},{19,3},{20,4},{21,5},{22,6},{23,7},{24,8},{25... | collective-permute-start | bytes 49160 | tf_op jit(solution)/shard_map/ppermute | solution.py:13
  270.3 2.1 collective-permute-start.3
Sparse Core Ops, SparseCore 0:
  19.1 79.4 reduce-scatter.2
  158.0 74.2 reduce-scatter.4
where the time goes:
time: 289 us; the launch traced here: 288 us
  waiting for transfers between devices  119 us (41%)
  blocking collectives  110 us (38%)
  matrix products  25.4 us (9%)
  between operations  16.4 us (6%)
  other arithmetic  7.89 us (3%)
  starting transfers between devices  5.42 us (2%)
  local copies, waits for them, and re-layouts  3.43 us (1%)
    reduce_scatter x2, waiting for transfers between devices, adjoint(): result = lax.psum_scatter(merged, 'dom', scatter_dimension=1, tiled=True)  115 us
    all_gather x2, blocking collectives, forward(): gathered = lax.all_gather(field, 'dom', axis=1, tiled=True)  73.3 us
    psum x1, blocking collectives, on_device(): lax.psum((local_primal, local_dual), ('section', 'dom'))  37.2 us
    dot_general x2, matrix products, forward(): jnp.einsum('prkij,prkj->pri', blocks, picked, precision=lax.Precision.HIG...  14.2 us
    dot_general x2, matrix products, adjoint(): jnp.einsum('prkij,pri->prkj', blocks, field_blocks, precision=lax.Precisi...  11.2 us
  transfers between devices with their start and end apart: 6, of which 6 were waited for; matrix products, arithmetic and copies ran while one was open for 0% of the time, Pallas kernels for 0%

commit v1 on v0

--- a/solution.py
+++ b/solution.py
@@ -24,7 +24,22 @@
 def forward(blocks, column_index, slot_index, field):
     periods_here = field.shape[0]
     width_here = blocks.shape[-1]
-    gathered = lax.all_gather(field, "dom", axis=1, tiled=True)
+    base_x = field
+    r2 = jax.lax.axis_size("dom")
+    out_arr, block_out, u1 = (r2, jax.lax.axis_index("dom"), base_x.shape[1])
+    gathered = lax.dynamic_update_slice_in_dim(
+        jnp.zeros(
+            [dd * out_arr if w == 1 else dd for w, dd in enumerate(base_x.shape)], base_x.dtype
+        ),
+        base_x,
+        block_out * u1,
+        axis=1,
+    )
+    for t in tuple(range(1, out_arr)):
+        base_x = jax.lax.ppermute(base_x, "dom", [(w, (w + 1) % out_arr) for w in range(out_arr)])
+        gathered = lax.dynamic_update_slice_in_dim(
+            gathered, base_x, (block_out - t) % out_arr * u1, axis=1
+        )
     carried = passed_along(gathered[-1:], "section", 1)
     stacked = jnp.concatenate([carried, gathered], axis=0)
     block_count = stacked.shape[1] // width_here

time: 289 us -> 432 us (1.49)
  waiting for transfers between devices: 119 us -> 335 us
  blocking collectives: 110 us -> 37.3 us
    ppermute x0 -> x30, waiting for transfers between devices: none -> 217 us  [forward(): jax.lax.ppermute(base_x, 'dom', [(w, (w + 1) % out_arr) for w in range(ou...]
    all_gather x2 -> x0, blocking collectives: 73.3 us -> none  [forward(): gathered = lax.all_gather(field, 'dom', axis=1, tiled=True)]
  transfers between devices with their start and end apart: 6 -> 36, of which waited for: 6 -> 36; matrix products, arithmetic and copies ran while one was open for 0% -> 0% of each run, Pallas kernels for 0% -> 0%
where the time goes in v1:
time: 432 us; the launch traced here: 431 us
  waiting for transfers between devices  335 us (78%)
  blocking collectives  37.3 us (9%)
  matrix products  25.3 us (6%)
  between operations  16.8 us (4%)
  other arithmetic  7.86 us (2%)
  starting transfers between devices  5.38 us (1%)
    ppermute x30, waiting for transfers between devices, forward(): jax.lax.ppermute(base_x, 'dom', [(w, (w + 1) % out_arr) for w in range(ou...  217 us
    reduce_scatter x2, waiting for transfers between devices, adjoint(): result = lax.psum_scatter(merged, 'dom', scatter_dimension=1, tiled=True)  113 us
    psum x1, blocking collectives, on_device(): lax.psum((local_primal, local_dual), ('section', 'dom'))  37.3 us
    dot_general x2, matrix products, forward(): jnp.einsum('prkij,prkj->pri', blocks, picked, precision=lax.Precision.HIG...  14.2 us
    dot_general x2, matrix products, adjoint(): jnp.einsum('prkij,pri->prkj', blocks, field_blocks, precision=lax.Precisi...  11.2 us
  transfers between devices with their start and end apart: 36, of which 36 were waited for; matrix products, arithmetic and copies ran while one was open for 0% of the time, Pallas kernels for 0%

profile of v1, /device:TPU:0, one launch (start us, length us, event | category | flops | bytes accessed | tf_op | source)
XLA Modules:
  0.0 431.2 jit_solution(10888004704596012410)
XLA Ops:
  7.2 0.7 fusion.14
  8.0 0.1 copy.12
  8.1 0.1 reshape.61
  8.2 6.1 %fusion.10 = f32[8,2,1,6,128]{4,2,3,1,0:T(1,128)S(1)} fusion(f32[8,2,6,128,128]{4,3,2,1,0:T(8,128)} %param.8, f32[8,2,128,1,1]{2,0,1,3,4:T(8,128)} %bitcast.58), kind=kOutput, calls=%fused_computation.24 | convolution fusion | flops 18874368 | bytes 6348800 | tf_op jit(solution)/shard_map/prkij,pri->prkj/dot_general | solution.py:57
  14.3 0.9 scatter_custom_fusion
  15.3 1.3 collective-permute-start
  16.6 1.7 collective-permute-done
  18.3 0.7 pad_add_fusion.1
  19.0 0.0 reduce-scatter.5.cloned.1.call-start
  19.9 78.8 %reduce-scatter.3.cloned.1.call-done = f32[8,256]{1,0:T(8,128)} async-done(((f32[8,4096]{1,0:T(8,128)}), f32[8,256]{1,0:T(8,128)}) %reduce-scatter.3.cloned.1.call-update) | async-done | bytes 8208 | tf_op jit(solution)/shard_map/reduce_scatter | solution.py:70
  98.7 1.3 multiply_reduce_fusion
  100.0 0.1 collective-permute-start.1
  100.3 7.0 %collective-permute-done.1 = f32[8,256]{1,0:T(8,128)S(1)} collective-permute-done((f32[8,256]{1,0:T(8,128)S(1)}, f32[8,256]{1,0:T(8,128)S(1)}, u32[]{:S(2)}, u32[]{:S(2)}) %collective-permute-start.1) | collective-permute-done | bytes 8224 | tf_op jit(solution)/shard_map/ppermute | solution.py:39
  107.3 7.2 %collective-permute-done.2 = f32[8,256]{1,0:T(8,128)S(1)} collective-permute-done((f32[8,256]{1,0:T(8,128)S(1)}, f32[8,256]{1,0:T(8,128)S(1)}, u32[]{:S(2)}, u32[]{:S(2)}) %collective-permute-start.2) | collective-permute-done | bytes 8224 | tf_op jit(solution)/shard_map/ppermute | solution.py:39
  114.6 7.2 %collective-permute-done.3 = f32[8,256]{1,0:T(8,128)S(1)} collective-permute-done((f32[8,256]{1,0:T(8,128)S(1)}, f32[8,256]{1,0:T(8,128)S(1)}, u32[]{:S(2)}, u32[]{:S(2)}) %collective-permute-start.3) | collective-permute-done | bytes 8224 | tf_op jit(solution)/shard_map/ppermute | solution.py:39
  121.8 7.2 %collective-permute-done.4 = f32[8,256]{1,0:T(8,128)S(1)} collective-permute-done((f32[8,256]{1,0:T(8,128)S(1)}, f32[8,256]{1,0:T(8,128)S(1)}, u32[]{:S(2)}, u32[]{:S(2)}) %collective-permute-start.4) | collective-permute-done | bytes 8224 | tf_op jit(solution)/shard_map/ppermute | solution.py:39
  129.1 7.2 %collective-permute-done.5 = f32[8,256]{1,0:T(8,128)S(1)} collective-permute-done((f32[8,256]{1,0:T(8,128)S(1)}, f32[8,256]{1,0:T(8,128)S(1)}, u32[]{:S(2)}, u32[]{:S(2)}) %collective-permute-start.5) | collective-permute-done | bytes 8224 | tf_op jit(solution)/shard_map/ppermute | solution.py:39
  136.3 7.2 %collective-permute-done.6 = f32[8,256]{1,0:T(8,128)S(1)} collective-permute-done((f32[8,256]{1,0:T(8,128)S(1)}, f32[8,256]{1,0:T(8,128)S(1)}, u32[]{:S(2)}, u32[]{:S(2)}) %collective-permute-start.6) | collective-permute-done | bytes 8224 | tf_op jit(solution)/shard_map/ppermute | solution.py:39
  143.6 7.2 %collective-permute-done.7 = f32[8,256]{1,0:T(8,128)S(1)} collective-permute-done((f32[8,256]{1,0:T(8,128)S(1)}, f32[8,256]{1,0:T(8,128)S(1)}, u32[]{:S(2)}, u32[]{:S(2)}) %collective-permute-start.7) | collective-permute-done | bytes 8224 | tf_op jit(solution)/shard_map/ppermute | solution.py:39
  150.8 7.2 %collective-permute-done.8 = f32[8,256]{1,0:T(8,128)S(1)} collective-permute-done((f32[8,256]{1,0:T(8,128)S(1)}, f32[8,256]{1,0:T(8,128)S(1)}, u32[]{:S(2)}, u32[]{:S(2)}) %collective-permute-start.8) | collective-permute-done | bytes 8224 | tf_op jit(solution)/shard_map/ppermute | solution.py:39
  158.1 7.2 %collective-permute-done.9 = f32[8,256]{1,0:T(8,128)S(1)} collective-permute-done((f32[8,256]{1,0:T(8,128)S(1)}, f32[8,256]{1,0:T(8,128)S(1)}, u32[]{:S(2)}, u32[]{:S(2)}) %collective-permute-start.9) | collective-permute-done | bytes 8224 | tf_op jit(solution)/shard_map/ppermute | solution.py:39
  165.3 7.2 %collective-permute-done.10 = f32[8,256]{1,0:T(8,128)S(1)} collective-permute-done((f32[8,256]{1,0:T(8,128)S(1)}, f32[8,256]{1,0:T(8,128)S(1)}, u32[]{:S(2)}, u32[]{:S(2)}) %collective-permute-start.10) | collective-permute-done | bytes 8224 | tf_op jit(solution)/shard_map/ppermute | solution.py:39
  172.6 7.2 %collective-permute-done.11 = f32[8,256]{1,0:T(8,128)S(1)} collective-permute-done((f32[8,256]{1,0:T(8,128)S(1)}, f32[8,256]{1,0:T(8,128)S(1)}, u32[]{:S(2)}, u32[]{:S(2)}) %collective-permute-start.11) | collective-permute-done | bytes 8224 | tf_op jit(solution)/shard_map/ppermute | solution.py:39
  179.8 7.2 %collective-permute-done.12 = f32[8,256]{1,0:T(8,128)S(1)} collective-permute-done((f32[8,256]{1,0:T(8,128)S(1)}, f32[8,256]{1,0:T(8,128)S(1)}, u32[]{:S(2)}, u32[]{:S(2)}) %collective-permute-start.12) | collective-permute-done | bytes 8224 | tf_op jit(solution)/shard_map/ppermute | solution.py:39
  187.1 7.2 %collective-permute-done.13 = f32[8,256]{1,0:T(8,128)S(1)} collective-permute-done((f32[8,256]{1,0:T(8,128)S(1)}, f32[8,256]{1,0:T(8,128)S(1)}, u32[]{:S(2)}, u32[]{:S(2)}) %collective-permute-start.13) | collective-permute-done | bytes 8224 | tf_op jit(solution)/shard_map/ppermute | solution.py:39
  194.3 7.2 %collective-permute-done.14 = f32[8,256]{1,0:T(8,128)S(1)} collective-permute-done((f32[8,256]{1,0:T(8,128)S(1)}, f32[8,256]{1,0:T(8,128)S(1)}, u32[]{:S(2)}, u32[]{:S(2)}) %collective-permute-start.14) | collective-permute-done | bytes 8224 | tf_op jit(solution)/shard_map/ppermute | solution.py:39
  201.6 7.2 %collective-permute-done.15 = f32[8,256]{1,0:T(8,128)S(1)} collective-permute-done((f32[8,256]{1,0:T(8,128)S(1)}, f32[8,256]{1,0:T(8,128)S(1)}, u32[]{:S(2)}, u32[]{:S(2)}) %collective-permute-start.15) | collective-permute-done | bytes 8224 | tf_op jit(solution)/shard_map/ppermute | solution.py:39
  208.8 1.3 collective-permute-start.16
  210.1 0.1 copy.13
  210.2 0.1 reshape.47
  210.3 0.6 collective-permute-done.16
  211.0 0.1 copy.22
  211.1 1.4 gather_fusion
  212.4 7.1 %fusion.18 = f32[8,2,1,128,1]{3,2,4,1,0:T(1,128)S(1)} fusion(f32[8,2,6,128,1]{3,4,2,1,0:T(1,128)S(1)} %bitcast.54, f32[8,2,6,128,128]{4,3,2,1,0:T(8,128)} %param.8), kind=kOutput, calls=%fused_computation.72 | convolution fusion | flops 18874368 | bytes 6348800 | tf_op jit(solution)/shard_map/prkij,prkj->pri/dot_general | solution.py:47
  219.6 0.6 multiply_reduce_fusion.1
  220.2 5.1 %fusion.8 = f32[8,2,1,6,128]{4,2,3,1,0:T(1,128)S(1)} fusion(f32[8,2,6,128,128]{4,3,2,1,0:T(8,128)} %param.8, f32[8,2,128,1,1]{2,0,1,3,4:T(8,128)S(1)} %bitcast.57), kind=kOutput, calls=%fused_computation.22 | convolution fusion | flops 18874368 | bytes 6348800 | tf_op jit(solution)/shard_map/prkij,pri->prkj/dot_general | solution.py:57
  225.2 0.9 scatter_custom_fusion.1
  226.2 1.3 collective-permute-start.17
  227.5 1.7 collective-permute-done.17
  229.3 0.7 pad_add_fusion
  230.0 37.3 %all-reduce.2 = (f32[]{:T(128)}, f32[]{:T(128)}) all-reduce(f32[]{:T(128)} %get-tuple-element.9, f32[]{:T(128)} %get-tuple-element.7), channel_id=1, replica_groups=mesh['section'=2,'dom'=16] {'section','dom'}, use_global_device_ids=true, to_apply=%region_3.4 | all-reduce | flops 2 | bytes 16 | tf_op jit(solution)/shard_map/psum | solution.py:91
  268.7 34.3 %reduce-scatter.5.cloned.1.call-done = f32[8,256]{1,0:T(8,128)} async-done(((f32[8,4096]{1,0:T(8,128)}), f32[8,256]{1,0:T(8,128)}) %reduce-scatter.5.cloned.1.call-update) | async-done | bytes 8208 | tf_op jit(solution)/shard_map/reduce_scatter | solution.py:70
  303.0 1.3 constant_dynamic-update-slice_fusion.15
  304.3 7.2 %collective-permute-done.18 = f32[8,256]{1,0:T(8,128)S(1)} collective-permute-done((f32[8,256]{1,0:T(8,128)S(1)}, f32[8,256]{1,0:T(8,128)S(1)}, u32[]{:S(2)}, u32[]{:S(2)}) %collective-permute-start.18) | collective-permute-done | bytes 8224 | tf_op jit(solution)/shard_map/ppermute | solution.py:39
  311.6 7.2 %collective-permute-done.19 = f32[8,256]{1,0:T(8,128)S(1)} collective-permute-done((f32[8,256]{1,0:T(8,128)S(1)}, f32[8,256]{1,0:T(8,128)S(1)}, u32[]{:S(2)}, u32[]{:S(2)}) %collective-permute-start.19) | collective-permute-done | bytes 8224 | tf_op jit(solution)/shard_map/ppermute | solution.py:39
  318.8 7.2 %collective-permute-done.20 = f32[8,256]{1,0:T(8,128)S(1)} collective-permute-done((f32[8,256]{1,0:T(8,128)S(1)}, f32[8,256]{1,0:T(8,128)S(1)}, u32[]{:S(2)}, u32[]{:S(2)}) %collective-permute-start.20) | collective-permute-done | bytes 8224 | tf_op jit(solution)/shard_map/ppermute | solution.py:39
  326.1 7.2 %collective-permute-done.21 = f32[8,256]{1,0:T(8,128)S(1)} collective-permute-done((f32[8,256]{1,0:T(8,128)S(1)}, f32[8,256]{1,0:T(8,128)S(1)}, u32[]{:S(2)}, u32[]{:S(2)}) %collective-permute-start.21) | collective-permute-done | bytes 8224 | tf_op jit(solution)/shard_map/ppermute | solution.py:39
  333.3 7.2 %collective-permute-done.22 = f32[8,256]{1,0:T(8,128)S(1)} collective-permute-done((f32[8,256]{1,0:T(8,128)S(1)}, f32[8,256]{1,0:T(8,128)S(1)}, u32[]{:S(2)}, u32[]{:S(2)}) %collective-permute-start.22) | collective-permute-done | bytes 8224 | tf_op jit(solution)/shard_map/ppermute | solution.py:39
  340.6 7.2 %collective-permute-done.23 = f32[8,256]{1,0:T(8,128)S(1)} collective-permute-done((f32[8,256]{1,0:T(8,128)S(1)}, f32[8,256]{1,0:T(8,128)S(1)}, u32[]{:S(2)}, u32[]{:S(2)}) %collective-permute-start.23) | collective-permute-done | bytes 8224 | tf_op jit(solution)/shard_map/ppermute | solution.py:39
  347.8 7.2 %collective-permute-done.24 = f32[8,256]{1,0:T(8,128)S(1)} collective-permute-done((f32[8,256]{1,0:T(8,128)S(1)}, f32[8,256]{1,0:T(8,128)S(1)}, u32[]{:S(2)}, u32[]{:S(2)}) %collective-permute-start.24) | collective-permute-done | bytes 8224 | tf_op jit(solution)/shard_map/ppermute | solution.py:39
  355.1 7.2 %collective-permute-done.25 = f32[8,256]{1,0:T(8,128)S(1)} collective-permute-done((f32[8,256]{1,0:T(8,128)S(1)}, f32[8,256]{1,0:T(8,128)S(1)}, u32[]{:S(2)}, u32[]{:S(2)}) %collective-permute-start.25) | collective-permute-done | bytes 8224 | tf_op jit(solution)/shard_map/ppermute | solution.py:39
  362.3 7.2 %collective-permute-done.26 = f32[8,256]{1,0:T(8,128)S(1)} collective-permute-done((f32[8,256]{1,0:T(8,128)S(1)}, f32[8,256]{1,0:T(8,128)S(1)}, u32[]{:S(2)}, u32[]{:S(2)}) %collective-permute-start.26) | collective-permute-done | bytes 8224 | tf_op jit(solution)/shard_map/ppermute | solution.py:39
  369.6 7.2 %collective-permute-done.27 = f32[8,256]{1,0:T(8,128)S(1)} collective-permute-done((f32[8,256]{1,0:T(8,128)S(1)}, f32[8,256]{1,0:T(8,128)S(1)}, u32[]{:S(2)}, u32[]{:S(2)}) %collective-permute-start.27) | collective-permute-done | bytes 8224 | tf_op jit(solution)/shard_map/ppermute | solution.py:39
  376.8 7.2 %collective-permute-done.28 = f32[8,256]{1,0:T(8,128)S(1)} collective-permute-done((f32[8,256]{1,0:T(8,128)S(1)}, f32[8,256]{1,0:T(8,128)S(1)}, u32[]{:S(2)}, u32[]{:S(2)}) %collective-permute-start.28) | collective-permute-done | bytes 8224 | tf_op jit(solution)/shard_map/ppermute | solution.py:39
  384.1 7.2 %collective-permute-done.29 = f32[8,256]{1,0:T(8,128)S(1)} collective-permute-done((f32[8,256]{1,0:T(8,128)S(1)}, f32[8,256]{1,0:T(8,128)S(1)}, u32[]{:S(2)}, u32[]{:S(2)}) %collective-permute-start.29) | collective-permute-done | bytes 8224 | tf_op jit(solution)/shard_map/ppermute | solution.py:39
  391.3 7.2 %collective-permute-done.30 = f32[8,256]{1,0:T(8,128)S(1)} collective-permute-done((f32[8,256]{1,0:T(8,128)S(1)}, f32[8,256]{1,0:T(8,128)S(1)}, u32[]{:S(2)}, u32[]{:S(2)}) %collective-permute-start.30) | collective-permute-done | bytes 8224 | tf_op jit(solution)/shard_map/ppermute | solution.py:39
  398.6 7.2 %collective-permute-done.31 = f32[8,256]{1,0:T(8,128)S(1)} collective-permute-done((f32[8,256]{1,0:T(8,128)S(1)}, f32[8,256]{1,0:T(8,128)S(1)}, u32[]{:S(2)}, u32[]{:S(2)}) %collective-permute-start.31) | collective-permute-done | bytes 8224 | tf_op jit(solution)/shard_map/ppermute | solution.py:39
  405.8 7.2 %collective-permute-done.32 = f32[8,256]{1,0:T(8,128)S(1)} collective-permute-done((f32[8,256]{1,0:T(8,128)S(1)}, f32[8,256]{1,0:T(8,128)S(1)}, u32[]{:S(2)}, u32[]{:S(2)}) %collective-permute-start.32) | collective-permute-done | bytes 8224 | tf_op jit(solution)/shard_map/ppermute | solution.py:39
  413.1 1.3 collective-permute-start.33
  414.4 0.8 collective-permute-done.33
  415.2 0.1 copy.23
  415.3 1.4 gather_fusion.1
  416.7 7.1 %fusion.19 = f32[8,2,1,128,1]{3,2,4,1,0:T(1,128)S(1)} fusion(f32[8,2,6,128,1]{3,4,2,1,0:T(1,128)S(1)} %bitcast.53, f32[8,2,6,128,128]{4,3,2,1,0:T(8,128)} %param.8), kind=kOutput, calls=%fused_computation.73 | convolution fusion | flops 18874368 | bytes 6348800 | tf_op jit(solution)/shard_map/prkij,prkj->pri/dot_general | solution.py:47
  423.8 0.6 fusion.5
  (90 shorter events, 0.5 us)
Async XLA Ops:
  7.2 91.5 %copy-start.2 = (f32[8,256]{1,0:T(8,128)S(1)}, f32[8,256]{1,0:T(8,128)}, u32[]{:S(2)}) copy-start(f32[8,256]{1,0:T(8,128)} %param.13) | copy-start | bytes 24580
  7.2 91.5 %copy-start.1 = (f32[8,256]{1,0:T(8,128)S(1)}, f32[8,256]{1,0:T(8,128)}, u32[]{:S(2)}) copy-start(f32[8,256]{1,0:T(8,128)} %param.11) | copy-start | bytes 24580
  7.2 91.5 %reduce-scatter.3.cloned.1.call-start = ((), (), s32[]{:S(2)}) async-start(), calls=%async_computation.2 | async-start | bytes 139264 | tf_op jit(solution)/shard_map/reduce_scatter | solution.py:70
  14.3 205.3 %copy-start = (f32[8,256]{1,0:T(8,128)S(1)}, f32[8,256]{1,0:T(8,128)}, u32[]{:S(2)}) copy-start(f32[8,256]{1,0:T(8,128)} %param.14) | copy-start | bytes 24580
  14.3 205.3 %copy-start.3 = (f32[8,256]{1,0:T(8,128)S(1)}, f32[8,256]{1,0:T(8,128)}, u32[]{:S(2)}) copy-start(f32[8,256]{1,0:T(8,128)} %param.12) | copy-start | bytes 24580
  15.3 3.1 collective-permute-start
  19.0 284.0 %reduce-scatter.5.cloned.1.call-start = ((), (), s32[]{:S(2)}) async-start(), calls=%async_computation.3 | async-start | bytes 139264 | tf_op jit(solution)/shard_map/reduce_scatter | solution.py:70
  100.0 7.3 %collective-permute-start.1 = (f32[8,256]{1,0:T(8,128)S(1)}, f32[8,256]{1,0:T(8,128)S(1)}, u32[]{:S(2)}, u32[]{:S(2)}) collective-permute-start(f32[8,256]{1,0:T(8,128)S(1)} %get-tuple-element.12), channel_id=1, source_target_pairs={{0,1},{1,2},{2,3},{3,4},{4,5},{5,6},{6,7},{7,8},{8,9},{9,10},{10,1... | collective-permute-start | bytes 24584 | tf_op jit(solution)/shard_map/ppermute | solution.py:39
  107.3 7.2 %collective-permute-start.2 = (f32[8,256]{1,0:T(8,128)S(1)}, f32[8,256]{1,0:T(8,128)S(1)}, u32[]{:S(2)}, u32[]{:S(2)}) collective-permute-start(f32[8,256]{1,0:T(8,128)S(1)} %collective-permute-done.1), channel_id=1, source_target_pairs={{0,1},{1,2},{2,3},{3,4},{4,5},{5,6},{6,7},{7,8},{8,9},{9,10},{10,1... | collective-permute-start | bytes 24584 | tf_op jit(solution)/shard_map/ppermute | solution.py:39
  114.6 7.2 %collective-permute-start.3 = (f32[8,256]{1,0:T(8,128)S(1)}, f32[8,256]{1,0:T(8,128)S(1)}, u32[]{:S(2)}, u32[]{:S(2)}) collective-permute-start(f32[8,256]{1,0:T(8,128)S(1)} %collective-permute-done.2), channel_id=1, source_target_pairs={{0,1},{1,2},{2,3},{3,4},{4,5},{5,6},{6,7},{7,8},{8,9},{9,10},{10,1... | collective-permute-start | bytes 24584 | tf_op jit(solution)/shard_map/ppermute | solution.py:39
  121.8 7.2 %collective-permute-start.4 = (f32[8,256]{1,0:T(8,128)S(1)}, f32[8,256]{1,0:T(8,128)S(1)}, u32[]{:S(2)}, u32[]{:S(2)}) collective-permute-start(f32[8,256]{1,0:T(8,128)S(1)} %collective-permute-done.3), channel_id=1, source_target_pairs={{0,1},{1,2},{2,3},{3,4},{4,5},{5,6},{6,7},{7,8},{8,9},{9,10},{10,1... | collective-permute-start | bytes 24584 | tf_op jit(solution)/shard_map/ppermute | solution.py:39
  129.1 7.2 %collective-permute-start.5 = (f32[8,256]{1,0:T(8,128)S(1)}, f32[8,256]{1,0:T(8,128)S(1)}, u32[]{:S(2)}, u32[]{:S(2)}) collective-permute-start(f32[8,256]{1,0:T(8,128)S(1)} %collective-permute-done.4), channel_id=1, source_target_pairs={{0,1},{1,2},{2,3},{3,4},{4,5},{5,6},{6,7},{7,8},{8,9},{9,10},{10,1... | collective-permute-start | bytes 24584 | tf_op jit(solution)/shard_map/ppermute | solution.py:39
  136.3 7.2 %collective-permute-start.6 = (f32[8,256]{1,0:T(8,128)S(1)}, f32[8,256]{1,0:T(8,128)S(1)}, u32[]{:S(2)}, u32[]{:S(2)}) collective-permute-start(f32[8,256]{1,0:T(8,128)S(1)} %collective-permute-done.5), channel_id=1, source_target_pairs={{0,1},{1,2},{2,3},{3,4},{4,5},{5,6},{6,7},{7,8},{8,9},{9,10},{10,1... | collective-permute-start | bytes 24584 | tf_op jit(solution)/shard_map/ppermute | solution.py:39
  143.6 7.2 %collective-permute-start.7 = (f32[8,256]{1,0:T(8,128)S(1)}, f32[8,256]{1,0:T(8,128)S(1)}, u32[]{:S(2)}, u32[]{:S(2)}) collective-permute-start(f32[8,256]{1,0:T(8,128)S(1)} %collective-permute-done.6), channel_id=1, source_target_pairs={{0,1},{1,2},{2,3},{3,4},{4,5},{5,6},{6,7},{7,8},{8,9},{9,10},{10,1... | collective-permute-start | bytes 24584 | tf_op jit(solution)/shard_map/ppermute | solution.py:39
  150.8 7.2 %collective-permute-start.8 = (f32[8,256]{1,0:T(8,128)S(1)}, f32[8,256]{1,0:T(8,128)S(1)}, u32[]{:S(2)}, u32[]{:S(2)}) collective-permute-start(f32[8,256]{1,0:T(8,128)S(1)} %collective-permute-done.7), channel_id=1, source_target_pairs={{0,1},{1,2},{2,3},{3,4},{4,5},{5,6},{6,7},{7,8},{8,9},{9,10},{10,1... | collective-permute-start | bytes 24584 | tf_op jit(solution)/shard_map/ppermute | solution.py:39
  158.1 7.2 %collective-permute-start.9 = (f32[8,256]{1,0:T(8,128)S(1)}, f32[8,256]{1,0:T(8,128)S(1)}, u32[]{:S(2)}, u32[]{:S(2)}) collective-permute-start(f32[8,256]{1,0:T(8,128)S(1)} %collective-permute-done.8), channel_id=1, source_target_pairs={{0,1},{1,2},{2,3},{3,4},{4,5},{5,6},{6,7},{7,8},{8,9},{9,10},{10,1... | collective-permute-start | bytes 24584 | tf_op jit(solution)/shard_map/ppermute | solution.py:39
  165.3 7.2 %collective-permute-start.10 = (f32[8,256]{1,0:T(8,128)S(1)}, f32[8,256]{1,0:T(8,128)S(1)}, u32[]{:S(2)}, u32[]{:S(2)}) collective-permute-start(f32[8,256]{1,0:T(8,128)S(1)} %collective-permute-done.9), channel_id=1, source_target_pairs={{0,1},{1,2},{2,3},{3,4},{4,5},{5,6},{6,7},{7,8},{8,9},{9,10},{10,1... | collective-permute-start | bytes 24584 | tf_op jit(solution)/shard_map/ppermute | solution.py:39
  172.6 7.2 %collective-permute-start.11 = (f32[8,256]{1,0:T(8,128)S(1)}, f32[8,256]{1,0:T(8,128)S(1)}, u32[]{:S(2)}, u32[]{:S(2)}) collective-permute-start(f32[8,256]{1,0:T(8,128)S(1)} %collective-permute-done.10), channel_id=1, source_target_pairs={{0,1},{1,2},{2,3},{3,4},{4,5},{5,6},{6,7},{7,8},{8,9},{9,10},{10,1... | collective-permute-start | bytes 24584 | tf_op jit(solution)/shard_map/ppermute | solution.py:39
  179.8 7.2 %collective-permute-start.12 = (f32[8,256]{1,0:T(8,128)S(1)}, f32[8,256]{1,0:T(8,128)S(1)}, u32[]{:S(2)}, u32[]{:S(2)}) collective-permute-start(f32[8,256]{1,0:T(8,128)S(1)} %collective-permute-done.11), channel_id=1, source_target_pairs={{0,1},{1,2},{2,3},{3,4},{4,5},{5,6},{6,7},{7,8},{8,9},{9,10},{10,1... | collective-permute-start | bytes 24584 | tf_op jit(solution)/shard_map/ppermute | solution.py:39
  187.1 7.2 %collective-permute-start.13 = (f32[8,256]{1,0:T(8,128)S(1)}, f32[8,256]{1,0:T(8,128)S(1)}, u32[]{:S(2)}, u32[]{:S(2)}) collective-permute-start(f32[8,256]{1,0:T(8,128)S(1)} %collective-permute-done.12), channel_id=1, source_target_pairs={{0,1},{1,2},{2,3},{3,4},{4,5},{5,6},{6,7},{7,8},{8,9},{9,10},{10,1... | collective-permute-start | bytes 24584 | tf_op jit(solution)/shard_map/ppermute | solution.py:39
  194.3 7.2 %collective-permute-start.14 = (f32[8,256]{1,0:T(8,128)S(1)}, f32[8,256]{1,0:T(8,128)S(1)}, u32[]{:S(2)}, u32[]{:S(2)}) collective-permute-start(f32[8,256]{1,0:T(8,128)S(1)} %collective-permute-done.13), channel_id=1, source_target_pairs={{0,1},{1,2},{2,3},{3,4},{4,5},{5,6},{6,7},{7,8},{8,9},{9,10},{10,1... | collective-permute-start | bytes 24584 | tf_op jit(solution)/shard_map/ppermute | solution.py:39
  201.5 7.2 %collective-permute-start.15 = (f32[8,256]{1,0:T(8,128)S(1)}, f32[8,256]{1,0:T(8,128)S(1)}, u32[]{:S(2)}, u32[]{:S(2)}) collective-permute-start(f32[8,256]{1,0:T(8,128)S(1)} %collective-permute-done.14), channel_id=1, source_target_pairs={{0,1},{1,2},{2,3},{3,4},{4,5},{5,6},{6,7},{7,8},{8,9},{9,10},{10,1... | collective-permute-start | bytes 24584 | tf_op jit(solution)/shard_map/ppermute | solution.py:39
  208.8 2.1 collective-permute-start.16
  226.2 3.1 collective-permute-start.17
  304.3 7.2 %collective-permute-start.18 = (f32[8,256]{1,0:T(8,128)S(1)}, f32[8,256]{1,0:T(8,128)S(1)}, u32[]{:S(2)}, u32[]{:S(2)}) collective-permute-start(f32[8,256]{1,0:T(8,128)S(1)} %get-tuple-element.5), channel_id=1, source_target_pairs={{0,1},{1,2},{2,3},{3,4},{4,5},{5,6},{6,7},{7,8},{8,9},{9,10},{10,1... | collective-permute-start | bytes 24584 | tf_op jit(solution)/shard_map/ppermute | solution.py:39
  311.6 7.2 %collective-permute-start.19 = (f32[8,256]{1,0:T(8,128)S(1)}, f32[8,256]{1,0:T(8,128)S(1)}, u32[]{:S(2)}, u32[]{:S(2)}) collective-permute-start(f32[8,256]{1,0:T(8,128)S(1)} %collective-permute-done.18), channel_id=1, source_target_pairs={{0,1},{1,2},{2,3},{3,4},{4,5},{5,6},{6,7},{7,8},{8,9},{9,10},{10,1... | collective-permute-start | bytes 24584 | tf_op jit(solution)/shard_map/ppermute | solution.py:39
  318.8 7.2 %collective-permute-start.20 = (f32[8,256]{1,0:T(8,128)S(1)}, f32[8,256]{1,0:T(8,128)S(1)}, u32[]{:S(2)}, u32[]{:S(2)}) collective-permute-start(f32[8,256]{1,0:T(8,128)S(1)} %collective-permute-done.19), channel_id=1, source_target_pairs={{0,1},{1,2},{2,3},{3,4},{4,5},{5,6},{6,7},{7,8},{8,9},{9,10},{10,1... | collective-permute-start | bytes 24584 | tf_op jit(solution)/shard_map/ppermute | solution.py:39
  326.1 7.2 %collective-permute-start.21 = (f32[8,256]{1,0:T(8,128)S(1)}, f32[8,256]{1,0:T(8,128)S(1)}, u32[]{:S(2)}, u32[]{:S(2)}) collective-permute-start(f32[8,256]{1,0:T(8,128)S(1)} %collective-permute-done.20), channel_id=1, source_target_pairs={{0,1},{1,2},{2,3},{3,4},{4,5},{5,6},{6,7},{7,8},{8,9},{9,10},{10,1... | collective-permute-start | bytes 24584 | tf_op jit(solution)/shard_map/ppermute | solution.py:39
  333.3 7.2 %collective-permute-start.22 = (f32[8,256]{1,0:T(8,128)S(1)}, f32[8,256]{1,0:T(8,128)S(1)}, u32[]{:S(2)}, u32[]{:S(2)}) collective-permute-start(f32[8,256]{1,0:T(8,128)S(1)} %collective-permute-done.21), channel_id=1, source_target_pairs={{0,1},{1,2},{2,3},{3,4},{4,5},{5,6},{6,7},{7,8},{8,9},{9,10},{10,1... | collective-permute-start | bytes 24584 | tf_op jit(solution)/shard_map/ppermute | solution.py:39
  340.6 7.2 %collective-permute-start.23 = (f32[8,256]{1,0:T(8,128)S(1)}, f32[8,256]{1,0:T(8,128)S(1)}, u32[]{:S(2)}, u32[]{:S(2)}) collective-permute-start(f32[8,256]{1,0:T(8,128)S(1)} %collective-permute-done.22), channel_id=1, source_target_pairs={{0,1},{1,2},{2,3},{3,4},{4,5},{5,6},{6,7},{7,8},{8,9},{9,10},{10,1... | collective-permute-start | bytes 24584 | tf_op jit(solution)/shard_map/ppermute | solution.py:39
  347.8 7.2 %collective-permute-start.24 = (f32[8,256]{1,0:T(8,128)S(1)}, f32[8,256]{1,0:T(8,128)S(1)}, u32[]{:S(2)}, u32[]{:S(2)}) collective-permute-start(f32[8,256]{1,0:T(8,128)S(1)} %collective-permute-done.23), channel_id=1, source_target_pairs={{0,1},{1,2},{2,3},{3,4},{4,5},{5,6},{6,7},{7,8},{8,9},{9,10},{10,1... | collective-permute-start | bytes 24584 | tf_op jit(solution)/shard_map/ppermute | solution.py:39
  355.1 7.2 %collective-permute-start.25 = (f32[8,256]{1,0:T(8,128)S(1)}, f32[8,256]{1,0:T(8,128)S(1)}, u32[]{:S(2)}, u32[]{:S(2)}) collective-permute-start(f32[8,256]{1,0:T(8,128)S(1)} %collective-permute-done.24), channel_id=1, source_target_pairs={{0,1},{1,2},{2,3},{3,4},{4,5},{5,6},{6,7},{7,8},{8,9},{9,10},{10,1... | collective-permute-start | bytes 24584 | tf_op jit(solution)/shard_map/ppermute | solution.py:39
  362.3 7.2 %collective-permute-start.26 = (f32[8,256]{1,0:T(8,128)S(1)}, f32[8,256]{1,0:T(8,128)S(1)}, u32[]{:S(2)}, u32[]{:S(2)}) collective-permute-start(f32[8,256]{1,0:T(8,128)S(1)} %collective-permute-done.25), channel_id=1, source_target_pairs={{0,1},{1,2},{2,3},{3,4},{4,5},{5,6},{6,7},{7,8},{8,9},{9,10},{10,1... | collective-permute-start | bytes 24584 | tf_op jit(solution)/shard_map/ppermute | solution.py:39
  369.6 7.2 %collective-permute-start.27 = (f32[8,256]{1,0:T(8,128)S(1)}, f32[8,256]{1,0:T(8,128)S(1)}, u32[]{:S(2)}, u32[]{:S(2)}) collective-permute-start(f32[8,256]{1,0:T(8,128)S(1)} %collective-permute-done.26), channel_id=1, source_target_pairs={{0,1},{1,2},{2,3},{3,4},{4,5},{5,6},{6,7},{7,8},{8,9},{9,10},{10,1... | collective-permute-start | bytes 24584 | tf_op jit(solution)/shard_map/ppermute | solution.py:39
  376.8 7.2 %collective-permute-start.28 = (f32[8,256]{1,0:T(8,128)S(1)}, f32[8,256]{1,0:T(8,128)S(1)}, u32[]{:S(2)}, u32[]{:S(2)}) collective-permute-start(f32[8,256]{1,0:T(8,128)S(1)} %collective-permute-done.27), channel_id=1, source_target_pairs={{0,1},{1,2},{2,3},{3,4},{4,5},{5,6},{6,7},{7,8},{8,9},{9,10},{10,1... | collective-permute-start | bytes 24584 | tf_op jit(solution)/shard_map/ppermute | solution.py:39
  384.1 7.2 %collective-permute-start.29 = (f32[8,256]{1,0:T(8,128)S(1)}, f32[8,256]{1,0:T(8,128)S(1)}, u32[]{:S(2)}, u32[]{:S(2)}) collective-permute-start(f32[8,256]{1,0:T(8,128)S(1)} %collective-permute-done.28), channel_id=1, source_target_pairs={{0,1},{1,2},{2,3},{3,4},{4,5},{5,6},{6,7},{7,8},{8,9},{9,10},{10,1... | collective-permute-start | bytes 24584 | tf_op jit(solution)/shard_map/ppermute | solution.py:39
  391.3 7.2 %collective-permute-start.30 = (f32[8,256]{1,0:T(8,128)S(1)}, f32[8,256]{1,0:T(8,128)S(1)}, u32[]{:S(2)}, u32[]{:S(2)}) collective-permute-start(f32[8,256]{1,0:T(8,128)S(1)} %collective-permute-done.29), channel_id=1, source_target_pairs={{0,1},{1,2},{2,3},{3,4},{4,5},{5,6},{6,7},{7,8},{8,9},{9,10},{10,1... | collective-permute-start | bytes 24584 | tf_op jit(solution)/shard_map/ppermute | solution.py:39
  398.6 7.2 %collective-permute-start.31 = (f32[8,256]{1,0:T(8,128)S(1)}, f32[8,256]{1,0:T(8,128)S(1)}, u32[]{:S(2)}, u32[]{:S(2)}) collective-permute-start(f32[8,256]{1,0:T(8,128)S(1)} %collective-permute-done.30), channel_id=1, source_target_pairs={{0,1},{1,2},{2,3},{3,4},{4,5},{5,6},{6,7},{7,8},{8,9},{9,10},{10,1... | collective-permute-start | bytes 24584 | tf_op jit(solution)/shard_map/ppermute | solution.py:39
  405.8 7.2 %collective-permute-start.32 = (f32[8,256]{1,0:T(8,128)S(1)}, f32[8,256]{1,0:T(8,128)S(1)}, u32[]{:S(2)}, u32[]{:S(2)}) collective-permute-start(f32[8,256]{1,0:T(8,128)S(1)} %collective-permute-done.31), channel_id=1, source_target_pairs={{0,1},{1,2},{2,3},{3,4},{4,5},{5,6},{6,7},{7,8},{8,9},{9,10},{10,1... | collective-permute-start | bytes 24584 | tf_op jit(solution)/shard_map/ppermute | solution.py:39
  413.1 2.1 collective-permute-start.33
Sparse Core Ops, SparseCore 0:
  19.1 79.4 reduce-scatter.2
  230.1 72.8 reduce-scatter.4
